TPU v7x, 1024 devices: a whole 4x8x16 slice. The times are simulated.
1024 devices in a mesh: row: 16 (over z), col: 64 (over y, x, core).
Axes of the slice: x: 4, y: 8, z: 16, core: 2. Of those that a mesh axis runs over, the one named last changes fastest.
Arguments:
- student_in: bfloat16 [512, 8192], P('col', 'row'), may hold values from -260 to 260
- teacher_hidden: bfloat16 [512, 16384], P(None, 'col'), may hold values from -1600 to 1600
- proj: bfloat16 [16384, 8192], P('col', 'row'), may hold values from -0.046875 to 0.046875
- w_gate: bfloat16 [8192, 28672], P('row', 'col'), may hold values from -0.0625 to 0.0625
- w_up: bfloat16 [8192, 28672], P('row', 'col'), may hold values from -0.0625 to 0.0625
- w_down: bfloat16 [28672, 8192], P('col', 'row'), may hold values from -0.03125 to 0.03125
Outputs:
- grad_gate: bfloat16 [8192, 28672], P('row', 'col')
- grad_up: bfloat16 [8192, 28672], P('row', 'col')
- grad_down: bfloat16 [28672, 8192], P('col', 'row')
- distill_loss: float32 [], replicated
All inputs are finite; a program needn't handle non-finite values.
Results may differ from a plain program's by a relative error of at most 0.0099.
Values may be sent and summed in bfloat16 or wider, within the bound.
A program may use at most 32 MiB of HBM per device.

v0:
```python
import jax
import jax.numpy as jnp
from jax import lax
from jax.sharding import PartitionSpec as P


def merged_2(array, axis, combine):
    everything = jax.tree.map(lambda part: lax.all_gather(part, axis), array)
    leading = jax.tree.map(lambda part: part[0], everything)

    def turn(k, so_far):
        return combine(so_far, jax.tree.map(lambda part: part[k], everything))

    return lax.fori_loop(1, lax.axis_size(axis), turn, leading)


def activate(gate_full, width_ff):
    gate_val = gate_full[:, :width_ff]
    up_val = gate_full[:, width_ff:]
    logistic = jax.nn.sigmoid(gate_val)
    silu_gate = gate_val * logistic
    hidden = (silu_gate * up_val).astype(jnp.bfloat16)
    return (gate_val, up_val, logistic, silu_gate, hidden)


def backward_pair(hidden_grad, gate_val, up_val, logistic, silu_gate):
    slope = logistic * (1.0 + gate_val * (1.0 - logistic))
    gate_grad = (hidden_grad * up_val * slope).astype(jnp.bfloat16)
    up_grad = (hidden_grad * silu_gate).astype(jnp.bfloat16)
    return jnp.concatenate([gate_grad, up_grad], axis=1)


def join_parts(first, second):
    stud_max = jnp.maximum(first[0], second[0])
    stud_norm = first[1] * jnp.exp(first[0] - stud_max) + second[1] * jnp.exp(second[0] - stud_max)
    teach_max = jnp.maximum(first[2], second[2])
    scale_one = jnp.exp(first[2] - teach_max)
    scale_two = jnp.exp(second[2] - teach_max)
    teach_norm = first[3] * scale_one + second[3] * scale_two
    cross_sum = first[4] * scale_one + second[4] * scale_two
    return (stud_max, stud_norm, teach_max, teach_norm, cross_sum)


def local(student_in, teacher_hidden, proj, w_gate, w_up, w_down):
    width_ff = w_gate.shape[1]
    tok_rows = lax.all_gather(student_in, "col", axis=0, tiled=True)
    gate_up = jnp.concatenate([w_gate, w_up], axis=1)
    gate_part = jnp.dot(tok_rows, gate_up, preferred_element_type=jnp.float32)
    gate_full = lax.psum(gate_part, "row")
    gate_val, up_val, logistic, silu_gate, hidden = activate(gate_full, width_ff)
    teach_part = jnp.dot(teacher_hidden, proj, preferred_element_type=jnp.float32)
    stud_part = jnp.dot(hidden, w_down, preferred_element_type=jnp.float32)
    stud_sum, teacher = lax.psum((stud_part, teach_part), "col")
    student = tok_rows.astype(jnp.float32) + stud_sum
    local_smax = jnp.max(student, axis=1)
    local_snorm = jnp.sum(jnp.exp(student - local_smax[:, None]), axis=1)
    local_tmax = jnp.max(teacher, axis=1)
    teach_exp = jnp.exp(teacher - local_tmax[:, None])
    local_tnorm = jnp.sum(teach_exp, axis=1)
    local_cross = jnp.sum(teach_exp * student, axis=1)
    merged = merged_2(
        (local_smax, local_snorm, local_tmax, local_tnorm, local_cross), "row", join_parts
    )
    stud_max, stud_norm, teach_max, teach_norm, cross_sum = merged
    token_loss = stud_max + jnp.log(stud_norm) - cross_sum / teach_norm
    stud_probs = jnp.exp(student - stud_max[:, None]) / stud_norm[:, None]
    teach_probs = jnp.exp(teacher - teach_max[:, None]) / teach_norm[:, None]
    stud_grad = (stud_probs - teach_probs).astype(jnp.bfloat16)
    distill_loss = jnp.mean(token_loss)
    grad_down = lax.dot_general(
        hidden, stud_grad, (((0,), (0,)), ((), ())), preferred_element_type=jnp.float32
    ).astype(jnp.bfloat16)
    hidden_part = lax.dot_general(
        stud_grad, w_down, (((1,), (1,)), ((), ())), preferred_element_type=jnp.float32
    )
    hidden_grad = lax.psum(hidden_part, "row")
    grad_pair = backward_pair(hidden_grad, gate_val, up_val, logistic, silu_gate)
    both_grads = lax.dot_general(
        tok_rows, grad_pair, (((0,), (0,)), ((), ())), preferred_element_type=jnp.float32
    ).astype(jnp.bfloat16)
    return (both_grads[:, :width_ff], both_grads[:, width_ff:], grad_down, distill_loss)


def solution(mesh):
    return jax.shard_map(
        local,
        mesh=mesh,
        in_specs=(
            P("col", "row"),
            P(None, "col"),
            P("col", "row"),
            P("row", "col"),
            P("row", "col"),
            P("col", "row"),
        ),
        out_specs=(P("row", "col"), P("row", "col"), P("col", "row"), P()),
        check_vma=False,
    )
```

profile of v0, /device:TPU:4, one launch (start us, length us, event | category | flops | bytes accessed | tf_op | source)
XLA Modules:
  0.0 812.3 jit_solution(18425732080016357265)
XLA Ops:
  7.2 58.9 %all_gather.33 = bf16[512,512]{1,0:T(8,128)(2,1)S(1)} all-gather(bf16[8,512]{1,0:T(8,128)(2,1)} %param.8), channel_id=1, replica_groups=mesh['row'=16,'col'=64] {'col'}, dimensions={0}, use_global_device_ids=true | all-gather | bytes 532480 | tf_op jit(solution)/shard_map/all_gather | solution.py:46
  66.1 3.1 convolution_bitcast_fusion
  69.3 1.3 fusion.14
  70.6 145.4 %all-reduce.5.cloned.1.call-done = f32[512,896]{0,1:T(8,128)} async-done(((f32[512,896]{0,1:T(8,128)}), f32[512,896]{0,1:T(8,128)}) %all-reduce.5.cloned.1.call-update) | async-done | bytes 1835024 | tf_op jit(solution)/shard_map/psum | solution.py:49
  216.0 1.7 multiply_convert_fusion.2
  217.7 1.5 fusion.13
  219.3 217.9 %all-reduce.9.cloned.1.call-done = (f32[512,512]{1,0:T(8,128)}, f32[512,512]{1,0:T(8,128)}) async-done(((f32[512,512]{1,0:T(8,128)}, f32[512,512]{1,0:T(8,128)}), (f32[512,512]{1,0:T(8,128)}, f32[512,512]{1,0:T(8,128)})) %all-reduce.9.cloned.1.call-update) | async-done | bytes 2097168 | tf_op jit(solution)/shard_map/psum | solution.py:53
  437.2 1.5 fusion.9
  439.8 31.5 %all-gather.8 = f32[16,1,512]{2,1,0:T(1,128)S(1)} all-gather(f32[1,1,512]{2,1,0:T(1,128)S(1)} %bitcast.74), channel_id=5, replica_groups=mesh['row'=16,'col'=64] {'row'}, dimensions={0}, use_global_device_ids=true | all-gather | bytes 34816 | tf_op jit(solution)/shard_map/all_gather | solution.py:8
  471.9 27.2 %all-gather.9 = f32[16,1,512]{2,1,0:T(1,128)S(1)} all-gather(f32[1,1,512]{2,1,0:T(1,128)S(1)} %bitcast.73), channel_id=6, replica_groups=mesh['row'=16,'col'=64] {'row'}, dimensions={0}, use_global_device_ids=true | all-gather | bytes 34816 | tf_op jit(solution)/shard_map/all_gather | solution.py:8
  500.3 28.0 %all-gather.6 = f32[16,1,512]{2,1,0:T(1,128)S(1)} all-gather(f32[1,1,512]{2,1,0:T(1,128)S(1)} %bitcast.72), channel_id=3, replica_groups=mesh['row'=16,'col'=64] {'row'}, dimensions={0}, use_global_device_ids=true | all-gather | bytes 34816 | tf_op jit(solution)/shard_map/all_gather | solution.py:8
  528.9 26.7 %all-gather.5 = f32[16,1,512]{2,1,0:T(1,128)S(1)} all-gather(f32[1,1,512]{2,1,0:T(1,128)S(1)} %bitcast.71), channel_id=2, replica_groups=mesh['row'=16,'col'=64] {'row'}, dimensions={0}, use_global_device_ids=true | all-gather | bytes 34816 | tf_op jit(solution)/shard_map/all_gather | solution.py:8
  556.2 27.5 %all-gather.7 = f32[16,1,512]{2,1,0:T(1,128)S(1)} all-gather(f32[1,1,512]{2,1,0:T(1,128)S(1)} %bitcast.70), channel_id=4, replica_groups=mesh['row'=16,'col'=64] {'row'}, dimensions={0}, use_global_device_ids=true | all-gather | bytes 34816 | tf_op jit(solution)/shard_map/all_gather | solution.py:8
  584.3 74.2 %while.23 = (s32[]{:T(128)}, f32[512]{0:T(512)S(1)}, f32[512]{0:T(512)S(1)}, f32[512]{0:T(512)S(1)}, f32[512]{0:T(512)S(1)}, /*index=5*/f32[512]{0:T(512)}, f32[...) while((s32[]{:T(128)}, f32[512]{0:T(512)S(1)}, ...), condition=%wide.region_9.0_spmd, body=%wide.region_8.0_spmd.sunk | while | flops 8709 | bytes 61635 | solution.py:14
  585.7 0.7 constant_dynamic-slice_fusion.12
  587.1 1.3 multiply_add_fusion.5
  589.2 0.7 constant_dynamic-slice_fusion.11
  590.7 0.7 constant_dynamic-slice_fusion.12
  592.1 1.3 multiply_add_fusion.5
  594.2 0.7 constant_dynamic-slice_fusion.11
  595.6 0.7 constant_dynamic-slice_fusion.12
  597.0 1.3 multiply_add_fusion.5
  599.1 0.7 constant_dynamic-slice_fusion.11
  600.6 0.7 constant_dynamic-slice_fusion.12
  602.0 1.3 multiply_add_fusion.5
  604.1 0.7 constant_dynamic-slice_fusion.11
  605.5 0.7 constant_dynamic-slice_fusion.12
  606.9 1.3 multiply_add_fusion.5
  609.0 0.7 constant_dynamic-slice_fusion.11
  610.5 0.7 constant_dynamic-slice_fusion.12
  611.9 1.3 multiply_add_fusion.5
  614.0 0.7 constant_dynamic-slice_fusion.11
  615.4 0.7 constant_dynamic-slice_fusion.12
  616.8 1.3 multiply_add_fusion.5
  618.9 0.7 constant_dynamic-slice_fusion.11
  620.4 0.7 constant_dynamic-slice_fusion.12
  621.8 1.3 multiply_add_fusion.5
  623.9 0.7 constant_dynamic-slice_fusion.11
  625.3 0.7 constant_dynamic-slice_fusion.12
  626.7 1.3 multiply_add_fusion.5
  628.8 0.7 constant_dynamic-slice_fusion.11
  630.3 0.7 constant_dynamic-slice_fusion.12
  631.7 1.3 multiply_add_fusion.5
  633.8 0.7 constant_dynamic-slice_fusion.11
  635.2 0.7 constant_dynamic-slice_fusion.12
  636.6 1.3 multiply_add_fusion.5
  638.7 0.7 constant_dynamic-slice_fusion.11
  640.2 0.7 constant_dynamic-slice_fusion.12
  641.6 1.3 multiply_add_fusion.5
  643.7 0.7 constant_dynamic-slice_fusion.11
  645.1 0.7 constant_dynamic-slice_fusion.12
  646.5 1.3 multiply_add_fusion.5
  648.6 0.7 constant_dynamic-slice_fusion.11
  650.1 0.7 constant_dynamic-slice_fusion.12
  651.5 1.3 multiply_add_fusion.5
  653.6 0.7 constant_dynamic-slice_fusion.11
  655.0 0.7 constant_dynamic-slice_fusion.12
  656.4 1.3 multiply_add_fusion.5
  659.1 0.8 copy-done.4
  659.9 1.4 fusion.15
  662.6 2.2 convolution_convert_fusion.1
  664.8 136.5 %all-reduce.7.cloned.1.call-done = f32[512,448]{0,1:T(8,128)} async-done(((f32[512,448]{0,1:T(8,128)}), f32[512,448]{0,1:T(8,128)}) %all-reduce.7.cloned.1.call-update) | async-done | bytes 917520 | tf_op jit(solution)/shard_map/psum | solution.py:76
  801.3 1.7 multiply_convert_fusion.1
  803.7 1.0 fusion.12
  (112 shorter events, 40.2 us)
Async XLA Ops:
  7.2 210.6 %copy-start = (bf16[448,512]{1,0:T(8,128)(2,1)S(1)}, bf16[448,512]{1,0:T(8,128)(2,1)}, u32[]{:S(2)}) copy-start(bf16[448,512]{1,0:T(8,128)(2,1)} %param.13) | copy-start | bytes 1376260
  7.2 208.8 %all-reduce.5.cloned.1.call-start = ((), (), s32[]{:S(2)}) async-start(), calls=%async_computation | async-start | bytes 3670016 | tf_op jit(solution)/shard_map/psum | solution.py:49
  66.1 3.2 copy-start.5
  66.1 3.2 copy-start.6
  69.2 367.9 %all-reduce.9.cloned.1.call-start = ((), (), s32[]{:S(2)}) async-start(), calls=%async_computation.2 | async-start | bytes 4194304 | tf_op jit(solution)/shard_map/psum | solution.py:53
  219.2 582.0 %all-reduce.7.cloned.1.call-start = ((), (), s32[]{:S(2)}) async-start(), calls=%async_computation.1 | async-start | bytes 1835008 | tf_op jit(solution)/shard_map/psum | solution.py:76
  437.2 1.6 copy-start.1
  437.2 1.9 copy-start.2
  659.1 0.8 copy-start.4
  659.9 1.4 copy-start.7
  659.9 141.4 %copy-start.3 = (f32[512,896]{0,1:T(8,128)S(1)}, f32[512,896]{0,1:T(8,128)}, u32[]{:S(2)}) copy-start(f32[512,896]{0,1:T(8,128)} %all-reduce.5.cloned.1.call-done) | copy-start | bytes 5505028
Sparse Core Ops, SparseCore 0:
  69.4 146.5 all-reduce.4
  219.9 217.2 all-reduce.8
  661.4 139.7 all-reduce.6
where the time goes:
time: 820 us; the launch traced here: 812 us
  waiting for transfers between devices  500 us (61%)
  blocking collectives  200 us (24%)
  local copies, waits for them, and re-layouts  59.9 us (7%)
  other arithmetic  26.7 us (3%)
  between operations  15.6 us (2%)
  matrix products  10.1 us (1%)
    psum x1, waiting for transfers between devices, local(): stud_sum, teacher = lax.psum((stud_part, teach_part), 'col')  218 us
    psum x1, waiting for transfers between devices, local(): gate_full = lax.psum(gate_part, 'row')  145 us
    all_gather x5, blocking collectives, merged_2(): everything = jax.tree.map(lambda part: lax.all_gather(part, axis), array)  141 us
    psum x1, waiting for transfers between devices, local(): hidden_grad = lax.psum(hidden_part, 'row')  136 us
    all_gather x1, blocking collectives, local(): tok_rows = lax.all_gather(student_in, 'col', axis=0, tiled=True)  58.9 us
    dynamic_slice x75, local copies, waits for them, and re-layouts, turn(): return combine(so_far, jax.tree.map(lambda part: part[k], everything))  54.2 us
    add x15, other arithmetic, join_parts(): cross_sum = first[4] * scale_one + second[4] * scale_two  19.3 us
  transfers between devices with their start and end apart: 3, of which 3 were waited for; matrix products, arithmetic and copies ran while one was open for 1% of the time, Pallas kernels for 0%

commit v1 on v0

v1 whole, which is shorter than its diff:
```python
import functools

import jax
import jax.numpy as jnp
from jax import lax
from jax.experimental import pallas as pl
from jax.experimental.pallas import tpu as pltpu
from jax.sharding import PartitionSpec as P

BF16 = jnp.bfloat16
F32 = jnp.float32
MESH = pl.DeviceIdType.MESH
DMA = pltpu.SemaphoreType.DMA
NSUB = 4
STOP = 99


def body(nz, ny, nx, si_h, th_h, proj_h, wg_h, wu_h, wd_h,
         gg_o, gu_o, gd_o, loss_o, s):
    zr = nz // 2
    zl = nz - 1 - zr
    tokens = ny * nx * 16
    grp = tokens // nz // 8
    ff = wg_h.shape[1]
    half = si_h.shape[1] // 2
    rows = 128 if tokens % 128 == 0 else tokens
    nrow = tokens // rows

    z = lax.axis_index("row")
    c = lax.axis_index("col")
    core = lax.rem(c, 2)
    other = 1 - core
    x = lax.rem(c // 2, nx)
    y = c // (2 * nx)

    def wrap(v, n):
        return lax.rem(v + 2 * n, n)

    def col(yy, xx, cc):
        return (yy * nx + xx) * 2 + cc

    partner = (z, col(y, x, other))
    right = (wrap(z + 1, nz), c)
    left = (wrap(z - 1, nz), c)

    def ypeer(d):
        return (z, col(wrap(y + d, ny), x, core))

    def xpeer(e):
        return (z, col(y, wrap(x + e, nx), core))

    def zpeer(d):
        return (wrap(z + d, nz), c)

    sent = []

    def send(src, dst, sems, at, device):
        send_sem, recv_sem = sems
        copy = pltpu.make_async_remote_copy(
            src_ref=src, dst_ref=dst, send_sem=send_sem.at[at], recv_sem=recv_sem.at[at],
            device_id=device, device_id_type=MESH)
        copy.start()
        sent.append(copy)
        return copy

    def flat(value):
        return value.reshape((-1, value.shape[-1]))

    loads = []
    for k, (src, dst) in enumerate((
            (si_h, s["si"]), (th_h, s["th"]), (proj_h, s["proj"]),
            (wg_h, s["wg"]), (wu_h, s["wu"]), (wd_h, s["wd"]))):
        copy = pltpu.make_async_copy(src, dst, s["load"].at[k])
        copy.start()
        loads.append(copy)

    barrier = pltpu.get_barrier_semaphore()
    greet = [partner, right, left]
    greet += [ypeer(d) for d in range(1, ny)] + [xpeer(e) for e in range(1, nx)]
    if nz > 3:
        greet += [zpeer(d) for d in range(2, nz - 1)]
    for device in greet:
        pl.semaphore_signal(barrier, inc=1, device_id=device, device_id_type=MESH)

    loads[0].wait()
    own = s["si"][...].astype(F32)
    s["pair_out"][...] = jnp.where(core == 0, own[:, half:], own[:, :half])
    s["pair"][core] = jnp.where(core == 0, own[:, :half], own[:, half:])
    pl.semaphore_wait(barrier, len(greet))
    pair_copy = send(s["pair_out"], s["pair"].at[core], s["pair_sem"], 0, partner)

    loads[1].wait()
    loads[2].wait()

    def teach_half(h):
        weights = s["proj"][:, pl.ds(pl.multiple_of(h * half, 128), half)]

        def tile(m, carry):
            start = pl.multiple_of(m * rows, rows)
            part = jnp.dot(s["th"][pl.ds(start, rows), :], weights, preferred_element_type=F32)
            s["tp"][h, pl.ds(m * (ny // nrow), ny // nrow)] = part.reshape((ny // nrow, nx, 16, half))
            return carry

        lax.fori_loop(0, nrow, tile, 0)

    def pair_stage(part, inbox, sems):
        return [send(part.at[other, :, wrap(x + e, nx)], inbox.at[:, wrap(x + e, nx)], sems, e, partner)
                for e in range(nx)]

    def x_stage(part, inbox, outbox, box, sems, pair_copies):
        copies = []
        for e in list(range(1, nx)) + [0]:
            group = wrap(x + e, nx)
            pair_copies[e].wait_recv()
            total = part[core, :, group] + inbox[:, group]
            if e == 0:
                outbox[0] = total
            else:
                outbox[e] = total
                copies.append(send(outbox.at[e], box.at[e - 1], sems, e - 1, xpeer(e)))
        return copies

    def y_stage(outbox, box, sums, ybox, sems, copies):
        for copy in copies:
            copy.wait_recv()
        total = outbox[0]
        for e in range(1, nx):
            total = total + box[e - 1]
        sums[...] = total
        return [send(sums.at[wrap(y + d, ny)], ybox.at[d - 1], sems, d - 1, ypeer(d)) for d in range(1, ny)]

    def y_total(sums, ybox, copies):
        for copy in copies:
            copy.wait_recv()
        total = sums[y]
        for d in range(1, ny):
            total = total + ybox[d - 1]
        return total

    teach_half(other)
    teach_pair = pair_stage(s["tp"], s["t_in"], s["tc_sem"])
    teach_half(core)

    def gather_start(buf, sems):
        y_sems, x_sems, _ = sems
        y_copies = [send(buf.at[core, y, x], buf.at[core, y, x], y_sems, d - 1, ypeer(d)) for d in range(1, ny)]
        x_copies = [[send(buf.at[core, y, x], buf.at[core, y, x], x_sems, e - 1, xpeer(e)) for e in range(1, nx)]]
        return y_copies, x_copies

    def gather_finish(buf, sems, started):
        y_copies, x_copies = started
        _, x_sems, c_sems = sems
        order = sorted(range(1, ny), key=lambda d: min(d, ny - d))
        for d in order:
            y_copies[d - 1].wait_recv()
            block = buf.at[core, wrap(y - d, ny), x]
            x_copies.append([send(block, block, x_sems, d * (nx - 1) + e - 1, xpeer(e)) for e in range(1, nx)])
        c_copies = [send(buf.at[core, :, x], buf.at[core, :, x], c_sems, 0, partner)]
        for e in sorted(range(1, nx), key=lambda e: min(e, nx - e)):
            for copies in x_copies:
                copies[e - 1].wait_recv()
            block = buf.at[core, :, wrap(x - e, nx)]
            c_copies.append(send(block, block, c_sems, e, partner))
        for copy in c_copies:
            copy.wait_recv()

    pair_copy.wait_recv()
    s["tok"][core, y, x] = flat(s["pair"][...]).astype(BF16)
    tok_sems = (s["ty_sem"], s["tx_sem"], s["tk_sem"])
    started = gather_start(s["tok"], tok_sems)
    loads[3].wait()
    loads[4].wait()
    s["wcat"][:, 0:ff] = s["wg"][...]
    s["wcat"][:, ff:2 * ff] = s["wu"][...]
    gather_finish(s["tok"], tok_sems, started)

    teach_x = x_stage(s["tp"], s["t_in"], s["t_out"], s["t_box"], s["txs_sem"], teach_pair)

    yrow = ny // nrow

    def gate_tile(m, carry):
        at = pl.ds(m * yrow, yrow)
        part = jnp.dot(flat(s["tok"][0, at]), s["wcat"][0:half, :], preferred_element_type=F32)
        part += jnp.dot(flat(s["tok"][1, at]), s["wcat"][half:2 * half, :], preferred_element_type=F32)
        s["gp"][pl.ds(m * (rows // 8), rows // 8)] = part.reshape((rows // 8, 8, 2 * ff))
        return carry

    lax.fori_loop(0, nrow, gate_tile, 0)

    def ring_reduce(part, rbox, lbox, sems, nsub, between):
        r_sems, l_sems = sems
        size = grp // nsub

        def chunk(j, q):
            return pl.ds(wrap(j, nz) * grp + q * size, size)

        def piece(q):
            return pl.ds(q * size, size)

        r_copies, l_copies = [], []
        for q in range(nsub):
            r_copies.append(send(part.at[chunk(z + zr, q)], rbox.at[0, piece(q)], r_sems, q, right))
            l_copies.append(send(part.at[chunk(z - zl, q)], lbox.at[0, piece(q)], l_sems, q, left))
        for step in range(1, zr):
            between(step)
            for q in range(nsub):
                r_copies[q].wait_recv()
                rbox[step - 1, piece(q)] = rbox[step - 1, piece(q)] + part[chunk(z + zr - step, q)]
                r_copies[q] = send(rbox.at[step - 1, piece(q)], rbox.at[step, piece(q)],
                                   r_sems, step * nsub + q, right)
                if step < zl:
                    l_copies[q].wait_recv()
                    lbox[step - 1, piece(q)] = lbox[step - 1, piece(q)] + part[chunk(z - zl + step, q)]
                    l_copies[q] = send(lbox.at[step - 1, piece(q)], lbox.at[step, piece(q)],
                                       l_sems, step * nsub + q, left)
        for q in range(nsub):
            l_copies[q].wait_recv()
            r_copies[q].wait_recv()
        total = part[pl.ds(z * grp, grp)] + rbox[zr - 1] + lbox[zl - 1]
        return flat(total)

    def ring_gather(buf, sems, between):
        r_sems, l_sems = sems
        r_copy = send(buf.at[z], buf.at[z], r_sems, 0, right)
        l_copy = send(buf.at[z], buf.at[z], l_sems, 0, left)
        for step in range(1, zr + 1):
            r_copy.wait_recv()
            if step < zr:
                block = buf.at[wrap(z - step, nz)]
                r_copy = send(block, block, r_sems, step, right)
            if step <= zl:
                l_copy.wait_recv()
                if step < zl:
                    block = buf.at[wrap(z + step, nz)]
                    l_copy = send(block, block, l_sems, step, left)
            between(step)

    y_copies = []

    def teach_between(step):
        if step == zr - 1:
            y_copies.extend(y_stage(s["t_out"], s["t_box"], s["t_sum"], s["t_ybox"], s["tys_sem"], teach_x))

    gate_up = ring_reduce(s["gp"], s["g_rbox"], s["g_lbox"], (s["gr_sem"], s["gl_sem"]), NSUB, teach_between)
    gate_val = gate_up[:, 0:ff]
    up_val = gate_up[:, ff:2 * ff]
    logistic = 1.0 / (1.0 + jnp.exp(-gate_val))
    silu_gate = gate_val * logistic
    s["hid"][z] = (silu_gate * up_val).astype(BF16)
    s["silu"][...] = silu_gate
    s["slope"][...] = up_val * (logistic * (1.0 + gate_val * (1.0 - logistic)))

    def teach_finish(step):
        if step == 1:
            s["teach"][...] = y_total(s["t_sum"], s["t_ybox"], y_copies)

    loads[5].wait()
    ring_gather(s["hid"], (s["hr_sem"], s["hl_sem"]), teach_finish)

    zrow = nz // nrow

    def stud_half(h):
        weights = s["wd"][:, pl.ds(pl.multiple_of(h * half, 128), half)]

        def tile(m, carry):
            part = jnp.dot(flat(s["hid"][pl.ds(m * zrow, zrow)]), weights, preferred_element_type=F32)
            s["sp"][h, pl.ds(m * yrow, yrow)] = part.reshape((yrow, nx, 16, half))
            return carry

        lax.fori_loop(0, nrow, tile, 0)

    stud_half(other)
    stud_pair = pair_stage(s["sp"], s["s_in"], s["sc_sem"])
    stud_half(core)
    stud_x = x_stage(s["sp"], s["s_in"], s["s_out"], s["s_box"], s["sxs_sem"], stud_pair)
    stud_y = y_stage(s["s_out"], s["s_box"], s["s_sum"], s["s_ybox"], s["sys_sem"], stud_x)

    teacher = s["teach"][...]
    teach_max = jnp.max(teacher, axis=1, keepdims=True)
    teach_exp = jnp.exp(teacher - teach_max)
    teach_norm = jnp.sum(teach_exp, axis=1, keepdims=True)

    student = flat(s["pair"][...]) + y_total(s["s_sum"], s["s_ybox"], stud_y)
    stud_max = jnp.max(student, axis=1, keepdims=True)
    stud_norm = jnp.sum(jnp.exp(student - stud_max), axis=1, keepdims=True)
    cross = jnp.sum(teach_exp * student, axis=1, keepdims=True)

    lane = lax.broadcasted_iota(jnp.int32, (16, 128), 1)
    stats = jnp.where(lane == 0, stud_max, jnp.where(lane == 1, teach_max, jnp.where(
        lane == 2, stud_norm, jnp.where(lane == 3, teach_norm, cross))))

    def join(tiles):
        top = functools.reduce(jnp.maximum, tiles)
        total = jnp.zeros((16, 128), F32)
        for tile in tiles:
            scale_s = jnp.exp(tile[:, 0:1] - top[:, 0:1])
            scale_t = jnp.exp(tile[:, 1:2] - top[:, 1:2])
            total += tile * jnp.where(lane == 2, scale_s, scale_t)
        return jnp.where(lane < 2, top, total)

    s["st_pair"][core] = stats
    send(s["st_pair"].at[core], s["st_pair"].at[core], s["stc_sem"], 0, partner).wait_recv()
    s["st_z"][z] = join([s["st_pair"][0], s["st_pair"][1]])
    st_copies = [send(s["st_z"].at[z], s["st_z"].at[z], s["stz_sem"], d - 1, zpeer(d)) for d in range(1, nz)]
    for copy in st_copies:
        copy.wait_recv()
    stats = join([s["st_z"][k] for k in range(nz)])
    stud_max = stats[:, 0:1]
    teach_max = stats[:, 1:2]
    stud_norm = stats[:, 2:3]
    teach_norm = stats[:, 3:4]
    cross = stats[:, 4:5]

    stud_grad = jnp.exp(student - stud_max) / stud_norm - jnp.exp(teacher - teach_max) / teach_norm
    s["sg"][core, y, x] = stud_grad.astype(BF16)
    sg_sems = (s["gy_sem"], s["gx_sem"], s["gk_sem"])
    started = gather_start(s["sg"], sg_sems)
    token_loss = stud_max + jnp.log(stud_norm) - cross / teach_norm
    own_loss = jnp.sum(token_loss, axis=0, keepdims=True) * (1.0 / tokens)
    s["ly"][y] = jnp.broadcast_to(own_loss, (8, 128))
    ly_copies = [send(s["ly"].at[y], s["ly"].at[y], s["ly_sem"], d - 1, ypeer(d)) for d in range(1, ny)]
    gather_finish(s["sg"], sg_sems, started)

    def grad_tile(m, carry):
        at = pl.ds(m * yrow, yrow)
        nt = (((1,), (1,)), ((), ()))
        part = lax.dot_general(flat(s["sg"][0, at]), s["wd"][:, 0:half], nt, preferred_element_type=F32)
        part += lax.dot_general(flat(s["sg"][1, at]), s["wd"][:, half:2 * half], nt, preferred_element_type=F32)
        s["hp"][pl.ds(m * (rows // 8), rows // 8)] = part.reshape((rows // 8, 8, ff))
        return carry

    lax.fori_loop(0, nrow, grad_tile, 0)

    tn = (((0,), (0,)), ((), ()))
    lx_copies = []

    def down_between(step):
        if step == 1:
            for h in range(2):
                s["gd"][:, h * half:(h + 1) * half] = lax.dot_general(
                    flat(s["hid"][...]), flat(s["sg"][h]), tn, preferred_element_type=F32).astype(BF16)
            out = pltpu.make_async_copy(s["gd"], gd_o, s["out"].at[0])
            out.start()
            loads.append(out)
        if step == min(2, zr - 1):
            for copy in ly_copies:
                copy.wait_recv()
            s["lx"][x] = functools.reduce(lambda a, b: a + b, [s["ly"][k] for k in range(ny)])
            lx_copies.extend(send(s["lx"].at[x], s["lx"].at[x], s["lx_sem"], e - 1, xpeer(e)) for e in range(1, nx))

    hidden_grad = ring_reduce(s["hp"], s["h_rbox"], s["h_lbox"], (s["pr_sem"], s["pl_sem"]),
                              min(2, grp), down_between)
    s["gr"][z, 0] = (hidden_grad * s["slope"][...]).astype(BF16)
    s["gr"][z, 1] = (hidden_grad * s["silu"][...]).astype(BF16)

    def loss_finish(step):
        if step == 1:
            for copy in lx_copies:
                copy.wait_recv()
            loss_o[...] = functools.reduce(lambda a, b: a + b, [s["lx"][k] for k in range(nx)])

    ring_gather(s["gr"], (s["wr_sem"], s["wl_sem"]), loss_finish)

    outs = []
    for k, (buf, dst) in enumerate(((s["gg"], gg_o), (s["gu"], gu_o))):
        grads = flat(s["gr"][:, k])
        for h in range(2):
            buf[h * half:(h + 1) * half, :] = lax.dot_general(
                flat(s["tok"][h]), grads, tn, preferred_element_type=F32).astype(BF16)
            at = pl.ds(h * half, half)
            out = pltpu.make_async_copy(buf.at[at], dst.at[at], s["out"].at[1 + 2 * k + h])
            out.start()
            outs.append(out)
    for copy in sent:
        copy.wait_send()
    loads[6].wait()
    for out in outs:
        out.wait()


def scratch(nz, ny, nx, d_in, k_in, ff):
    zr = nz // 2
    zl = nz - 1 - zr
    tokens = ny * nx * 16
    half = d_in // 2
    tz = tokens // nz
    g = tz // 8
    V = pltpu.VMEM

    def sems(*n):
        return (DMA(n), DMA(n))

    vm = dict(
        si=V((8, d_in), BF16), th=V((tokens, k_in), BF16), proj=V((k_in, d_in), BF16),
        wg=V((d_in, ff), BF16), wu=V((d_in, ff), BF16), wd=V((ff, d_in), BF16),
        wcat=V((d_in, 2 * ff), BF16),
        pair_out=V((8, half), F32), pair=V((2, 8, half), F32),
        tok=V((2, ny, nx, 16, half), BF16), sg=V((2, ny, nx, 16, half), BF16),
        tp=V((2, ny, nx, 16, half), F32), sp=V((2, ny, nx, 16, half), F32),
        t_in=V((ny, nx, 16, half), F32), s_in=V((ny, nx, 16, half), F32),
        t_out=V((nx, ny, 16, half), F32), s_out=V((nx, ny, 16, half), F32),
        t_box=V((nx - 1, ny, 16, half), F32), s_box=V((nx - 1, ny, 16, half), F32),
        t_sum=V((ny, 16, half), F32), s_sum=V((ny, 16, half), F32),
        t_ybox=V((ny - 1, 16, half), F32), s_ybox=V((ny - 1, 16, half), F32),
        teach=V((16, half), F32),
        gp=V((tokens // 8, 8, 2 * ff), F32), hp=V((tokens // 8, 8, ff), F32),
        g_rbox=V((zr, g, 8, 2 * ff), F32), g_lbox=V((zl, g, 8, 2 * ff), F32),
        h_rbox=V((zr, g, 8, ff), F32), h_lbox=V((zl, g, 8, ff), F32),
        hid=V((nz, tz, ff), BF16), gr=V((nz, 2, tz, ff), BF16),
        silu=V((tz, ff), F32), slope=V((tz, ff), F32),
        st_pair=V((2, 16, 128), F32), st_z=V((nz, 16, 128), F32),
        ly=V((ny, 8, 128), F32), lx=V((nx, 8, 128), F32),
        gd=V((ff, d_in), BF16), gg=V((d_in, ff), BF16), gu=V((d_in, ff), BF16),
    )
    gs, hs = NSUB, min(2, g)
    sm = dict(
        pair_sem=sems(1), tc_sem=sems(nx), sc_sem=sems(nx),
        txs_sem=sems(nx - 1), sxs_sem=sems(nx - 1), tys_sem=sems(ny - 1), sys_sem=sems(ny - 1),
        ty_sem=sems(ny - 1), tx_sem=sems(ny * (nx - 1)), tk_sem=sems(nx),
        gy_sem=sems(ny - 1), gx_sem=sems(ny * (nx - 1)), gk_sem=sems(nx),
        gr_sem=sems(zr * gs), gl_sem=sems(zl * gs), hr_sem=sems(zr), hl_sem=sems(zl),
        pr_sem=sems(zr * hs), pl_sem=sems(zl * hs), wr_sem=sems(zr), wl_sem=sems(zl),
        stc_sem=sems(1), stz_sem=sems(nz - 1), ly_sem=sems(ny - 1), lx_sem=sems(nx - 1),
        load=DMA((6,)), out=DMA((5,)),
    )
    return {**vm, **sm}


def local(nz, ny, nx, student_in, teacher_hidden, proj, w_gate, w_up, w_down):
    d_in = student_in.shape[1]
    ff = w_gate.shape[1]
    names = scratch(nz, ny, nx, d_in, proj.shape[0], ff)
    tree = jax.tree.structure(names)
    leaves = jax.tree.leaves(names)

    def kernel(*refs):
        s = jax.tree.unflatten(tree, refs[10:])
        body(nz, ny, nx, *refs[:10], s)

    any_spec = pl.BlockSpec(memory_space=pl.ANY)
    out = pl.pallas_call(
        kernel,
        out_shape=(
            jax.ShapeDtypeStruct((d_in, ff), BF16), jax.ShapeDtypeStruct((d_in, ff), BF16),
            jax.ShapeDtypeStruct((ff, d_in), BF16), jax.ShapeDtypeStruct((8, 128), F32)),
        in_specs=[any_spec] * 6,
        out_specs=(any_spec, any_spec, any_spec, pl.BlockSpec(memory_space=pltpu.VMEM)),
        scratch_shapes=leaves,
        compiler_params=pltpu.CompilerParams(
            collective_id=0, has_side_effects=True, vmem_limit_bytes=56 * 1024 * 1024),
        name="distill_step",
    )(student_in, teacher_hidden, proj, w_gate, w_up, w_down)
    return out[0], out[1], out[2], out[3][0, 0]


def solution(mesh):
    nz = mesh.shape["row"]
    chips = mesh.shape["col"] // 2
    nx = 4 if chips == 32 else 2
    ny = chips // nx
    return jax.shard_map(
        functools.partial(local, nz, ny, nx),
        mesh=mesh,
        in_specs=(
            P("col", "row"),
            P(None, "col"),
            P("col", "row"),
            P("row", "col"),
            P("row", "col"),
            P("col", "row"),
        ),
        out_specs=(P("row", "col"), P("row", "col"), P("col", "row"), P()),
        check_vma=False,
    )
```

time: 820 us -> 197 us (0.24)
  the two profiles are of different devices: /device:TPU:4 before, /device:TPU:8 now
where the time goes in v1:
time: 197 us
  Pallas kernels  188 us (95%)
  local copies, waits for them, and re-layouts  8.1 us (4%)
    pallas_call x1, Pallas kernels, local(): pl.pallas_call(kernel, out_shape=(jax.ShapeDtypeStruct((d_in, ff), BF16),...  188 us
    unnamed x11, local copies, waits for them, and re-layouts  6.86 us

profile of v1, /device:TPU:8, one launch (start us, length us, event | category | flops | bytes accessed | tf_op | source)
XLA Modules:
  0.0 196.5 jit_solution(6127471791101478664)
XLA Ops:
  0.6 0.0 copy-start.2
  0.6 2.1 %copy.10.refs_3_ = bf16[512,448]{1,0:T(8,128)(2,1)} copy(bf16[512,448]{0,1:T(8,128)(2,1)} %param.9) | data formatting | bytes 917504 | tf_op args[3]
  2.7 0.0 copy-done.2
  2.7 1.0 copy.11.refs_4_
  3.7 187.8 %distill_step.1 = (bf16[512,448]{1,0:T(8,128)(2,1)}, bf16[512,448]{1,0:T(8,128)(2,1)}, bf16[448,512]{1,0:T(8,128)(2,1)}, f32[8,128]{1,0:T(8,128)}) custom-call(bf16[8,512]{1,0:T(8,128)(2,1)} %refs_0_.1, bf16[512,256]{1,0:T(8,128)(2,1)} %refs_1_.1, bf16[256,512]{1,0:T(8,128)(2,1)} %refs_2_.1, bf16[512,448]{1,0:T(8,128)(2,1)} %copy.10.refs_3_, ...), custom_call_target="tpu_custom_call" | custom-call | tf_op jit(solution)/shard_map/distill_step/pallas_call | solution.py:441
  191.5 0.0 copy-start
  191.5 1.2 slice.3
  192.8 2.0 %copy.12 = bf16[512,448]{0,1:T(8,128)(2,1)} copy(bf16[512,448]{1,0:T(8,128)(2,1)} %get-tuple-element.12) | data formatting | bytes 917504
  194.8 0.0 copy-done
  194.8 0.0 copy-start.1
  194.8 1.0 copy.13
  195.7 0.1 copy-done.1
  195.8 0.8 copy.15
Async XLA Ops:
  0.6 2.1 %copy-start.2 = (bf16[512,448]{0,1:T(8,128)(2,1)S(1)}, bf16[512,448]{0,1:T(8,128)(2,1)}, u32[]{:S(2)}) copy-start(bf16[512,448]{0,1:T(8,128)(2,1)} %param.10) | copy-start | bytes 1376260
  191.5 3.3 %copy-start = (bf16[512,448]{1,0:T(8,128)(2,1)S(1)}, bf16[512,448]{1,0:T(8,128)(2,1)}, u32[]{:S(2)}) copy-start(bf16[512,448]{1,0:T(8,128)(2,1)} %get-tuple-element.13) | copy-start | bytes 1376260
  194.8 1.0 copy-start.1

commit v2 on v1

--- a/solution.py
+++ b/solution.py
@@ -12,7 +12,7 @@
 MESH = pl.DeviceIdType.MESH
 DMA = pltpu.SemaphoreType.DMA
 NSUB = 4
-STOP = 99
+WSUB = 2
 
 
 def body(nz, ny, nx, si_h, th_h, proj_h, wg_h, wu_h, wd_h,
@@ -21,7 +21,9 @@
     zl = nz - 1 - zr
     tokens = ny * nx * 16
     grp = tokens // nz // 8
-    ff = wg_h.shape[1]
+    tg = tokens // nz // 16
+    ff = wg_h.shape[0]
+    ffp = s["wd"].shape[0]
     half = si_h.shape[1] // 2
     rows = 128 if tokens % 128 == 0 else tokens
     nrow = tokens // rows
@@ -69,7 +71,7 @@
     loads = []
     for k, (src, dst) in enumerate((
             (si_h, s["si"]), (th_h, s["th"]), (proj_h, s["proj"]),
-            (wg_h, s["wg"]), (wu_h, s["wu"]), (wd_h, s["wd"]))):
+            (wg_h, s["wcat"].at[0:ff]), (wu_h, s["wcat"].at[ff:2 * ff]), (wd_h, s["wd"].at[0:ff]))):
         copy = pltpu.make_async_copy(src, dst, s["load"].at[k])
         copy.start()
         loads.append(copy)
@@ -77,10 +79,13 @@
     barrier = pltpu.get_barrier_semaphore()
     greet = [partner, right, left]
     greet += [ypeer(d) for d in range(1, ny)] + [xpeer(e) for e in range(1, nx)]
-    if nz > 3:
-        greet += [zpeer(d) for d in range(2, nz - 1)]
+    greet += [zpeer(d) for d in sorted({2, nz - 2} - {1})]
     for device in greet:
         pl.semaphore_signal(barrier, inc=1, device_id=device, device_id_type=MESH)
+
+    if ffp > ff:
+        s["wd"][ff:ffp, :] = jnp.zeros((ffp - ff, 2 * half), BF16)
+        s["hid"][z, :, ff:ffp] = jnp.zeros((s["hid"].shape[1], ffp - ff), BF16)
 
     loads[0].wait()
     own = s["si"][...].astype(F32)
@@ -168,20 +173,19 @@
     s["tok"][core, y, x] = flat(s["pair"][...]).astype(BF16)
     tok_sems = (s["ty_sem"], s["tx_sem"], s["tk_sem"])
     started = gather_start(s["tok"], tok_sems)
+    gather_finish(s["tok"], tok_sems, started)
+
+    teach_x = x_stage(s["tp"], s["t_in"], s["t_out"], s["t_box"], s["txs_sem"], teach_pair)
+
     loads[3].wait()
     loads[4].wait()
-    s["wcat"][:, 0:ff] = s["wg"][...]
-    s["wcat"][:, ff:2 * ff] = s["wu"][...]
-    gather_finish(s["tok"], tok_sems, started)
-
-    teach_x = x_stage(s["tp"], s["t_in"], s["t_out"], s["t_box"], s["txs_sem"], teach_pair)
-
     yrow = ny // nrow
+    nt = (((1,), (1,)), ((), ()))
 
     def gate_tile(m, carry):
         at = pl.ds(m * yrow, yrow)
-        part = jnp.dot(flat(s["tok"][0, at]), s["wcat"][0:half, :], preferred_element_type=F32)
-        part += jnp.dot(flat(s["tok"][1, at]), s["wcat"][half:2 * half, :], preferred_element_type=F32)
+        part = lax.dot_general(flat(s["tok"][0, at]), s["wcat"][:, 0:half], nt, preferred_element_type=F32)
+        part += lax.dot_general(flat(s["tok"][1, at]), s["wcat"][:, half:2 * half], nt, preferred_element_type=F32)
         s["gp"][pl.ds(m * (rows // 8), rows // 8)] = part.reshape((rows // 8, 8, 2 * ff))
         return carry
 
@@ -219,21 +223,92 @@
         total = part[pl.ds(z * grp, grp)] + rbox[zr - 1] + lbox[zl - 1]
         return flat(total)
 
-    def ring_gather(buf, sems, between):
+    def ring_gather(buf, sems, nsub, between):
         r_sems, l_sems = sems
-        r_copy = send(buf.at[z], buf.at[z], r_sems, 0, right)
-        l_copy = send(buf.at[z], buf.at[z], l_sems, 0, left)
+        size = buf.shape[1] // nsub
+
+        def part(k, q):
+            return buf.at[k, pl.ds(q * size, size)]
+
+        r_copies, l_copies = [], []
+        for q in range(nsub):
+            r_copies.append(send(part(z, q), part(z, q), r_sems, q, right))
+            l_copies.append(send(part(z, q), part(z, q), l_sems, q, left))
         for step in range(1, zr + 1):
-            r_copy.wait_recv()
-            if step < zr:
-                block = buf.at[wrap(z - step, nz)]
-                r_copy = send(block, block, r_sems, step, right)
-            if step <= zl:
-                l_copy.wait_recv()
-                if step < zl:
-                    block = buf.at[wrap(z + step, nz)]
-                    l_copy = send(block, block, l_sems, step, left)
+            for q in range(nsub):
+                r_copies[q].wait_recv()
+                if step < zr:
+                    block = part(wrap(z - step, nz), q)
+                    r_copies[q] = send(block, block, r_sems, step * nsub + q, right)
+                if step <= zl:
+                    l_copies[q].wait_recv()
+                    if step < zl:
+                        block = part(wrap(z + step, nz), q)
+                        l_copies[q] = send(block, block, l_sems, step * nsub + q, left)
             between(step)
+
+    def skip_gather(buf, sems, between):
+        copies = [{}, {}]
+        sides = ((0, 1, zr), (1, -1, zl))
+
+        def spread(side, sign, reach, distance):
+            block = buf.at[wrap(z - sign * distance, nz)]
+            for hop in (2, 1):
+                if distance + hop <= reach:
+                    copies[side][distance + hop] = send(
+                        block, block, sems[side], distance + hop - 1, zpeer(sign * hop))
+
+        for side in sides:
+            spread(*side, 0)
+        for distance in range(2, zr + 1, 2):
+            for side, sign, reach in sides:
+                if distance <= reach:
+                    copies[side][distance].wait_recv()
+                    spread(side, sign, reach, distance)
+            between(distance // 2)
+        for side, sign, reach in sides:
+            for distance in range(1, reach + 1, 2):
+                copies[side][distance].wait_recv()
+
+    def skip_reduce(part, stage, boxes, sems, between):
+        copies = [{}, {}]
+        sides = ((0, 1, zr), (1, -1, zl))
+
+        def own(j):
+            return part[pl.ds(wrap(j, nz) * tg, tg)]
+
+        def arrived(side, reach, distance):
+            total = 0.0
+            for hop in (1, 2):
+                if distance + hop <= reach:
+                    copies[side][distance + hop].wait_recv()
+                    total = total + boxes[side][distance + hop - 1].astype(F32)
+            return total
+
+        def launch(side, sign, distance, value):
+            hop = 2 - distance % 2
+            stage[side, distance - 1] = value.astype(BF16)
+            copies[side][distance] = send(
+                stage.at[side, distance - 1], boxes[side].at[distance - 1], sems[side], distance - 1, zpeer(sign * hop))
+
+        for side, sign, reach in sides:
+            if reach % 2 == 0:
+                launch(side, sign, reach, own(z + sign * reach))
+        for distance in range(zr - 1 + zr % 2, 0, -2):
+            for side, sign, reach in sides:
+                if distance <= reach:
+                    launch(side, sign, distance, own(z + sign * distance))
+        step = 0
+        for distance in range(zr, 1, -2):
+            step += 1
+            for side, sign, reach in sides:
+                if distance < reach:
+                    launch(side, sign, distance, own(z + sign * distance) + arrived(side, reach, distance))
+            between(step)
+        total = own(z)
+        for side, sign, reach in sides:
+            total = total + arrived(side, reach, 0)
+        return flat(total)
 
     y_copies = []
 
@@ -246,7 +321,7 @@
     up_val = gate_up[:, ff:2 * ff]
     logistic = 1.0 / (1.0 + jnp.exp(-gate_val))
     silu_gate = gate_val * logistic
-    s["hid"][z] = (silu_gate * up_val).astype(BF16)
+    s["hid"][z, :, 0:ff] = (silu_gate * up_val).astype(BF16)
     s["silu"][...] = silu_gate
     s["slope"][...] = up_val * (logistic * (1.0 + gate_val * (1.0 - logistic)))
 
@@ -255,7 +330,7 @@
             s["teach"][...] = y_total(s["t_sum"], s["t_ybox"], y_copies)
 
     loads[5].wait()
-    ring_gather(s["hid"], (s["hr_sem"], s["hl_sem"]), teach_finish)
+    skip_gather(s["hid"], (s["hr_sem"], s["hl_sem"]), teach_finish)
 
     zrow = nz // nrow
 
@@ -288,15 +363,16 @@
     lane = lax.broadcasted_iota(jnp.int32, (16, 128), 1)
     stats = jnp.where(lane == 0, stud_max, jnp.where(lane == 1, teach_max, jnp.where(
         lane == 2, stud_norm, jnp.where(lane == 3, teach_norm, cross))))
+    stats = jnp.concatenate([stats, jnp.zeros((112, 128), F32)], axis=0).T[0:8]
+    row = lax.broadcasted_iota(jnp.int32, (8, 128), 0)
 
     def join(tiles):
         top = functools.reduce(jnp.maximum, tiles)
-        total = jnp.zeros((16, 128), F32)
+        total = jnp.zeros((8, 128), F32)
         for tile in tiles:
-            scale_s = jnp.exp(tile[:, 0:1] - top[:, 0:1])
-            scale_t = jnp.exp(tile[:, 1:2] - top[:, 1:2])
-            total += tile * jnp.where(lane == 2, scale_s, scale_t)
-        return jnp.where(lane < 2, top, total)
+            scale = jnp.exp(tile - top)
+            total += tile * jnp.where(row == 2, scale[0:1], scale[1:2])
+        return jnp.where(row < 2, top, total)
 
     s["st_pair"][core] = stats
     send(s["st_pair"].at[core], s["st_pair"].at[core], s["stc_sem"], 0, partner).wait_recv()
@@ -305,6 +381,7 @@
     for copy in st_copies:
         copy.wait_recv()
     stats = join([s["st_z"][k] for k in range(nz)])
+    stats = jnp.concatenate([stats, jnp.zeros((120, 128), F32)], axis=0).T[0:16]
     stud_max = stats[:, 0:1]
     teach_max = stats[:, 1:2]
     stud_norm = stats[:, 2:3]
@@ -323,10 +400,9 @@
 
     def grad_tile(m, carry):
         at = pl.ds(m * yrow, yrow)
-        nt = (((1,), (1,)), ((), ()))
         part = lax.dot_general(flat(s["sg"][0, at]), s["wd"][:, 0:half], nt, preferred_element_type=F32)
         part += lax.dot_general(flat(s["sg"][1, at]), s["wd"][:, half:2 * half], nt, preferred_element_type=F32)
-        s["hp"][pl.ds(m * (rows // 8), rows // 8)] = part.reshape((rows // 8, 8, ff))
+        s["hp"][pl.ds(m * (rows // 16), rows // 16)] = part.reshape((rows // 16, 16, ffp))
         return carry
 
     lax.fori_loop(0, nrow, grad_tile, 0)
@@ -338,39 +414,39 @@
         if step == 1:
             for h in range(2):
                 s["gd"][:, h * half:(h + 1) * half] = lax.dot_general(
-                    flat(s["hid"][...]), flat(s["sg"][h]), tn, preferred_element_type=F32).astype(BF16)
+                    flat(s["hid"][...]), flat(s["sg"][h]), tn, preferred_element_type=F32).astype(BF16)[0:ff]
             out = pltpu.make_async_copy(s["gd"], gd_o, s["out"].at[0])
             out.start()
             loads.append(out)
-        if step == min(2, zr - 1):
+        if step == max(1, zr // 2 - 1):
             for copy in ly_copies:
                 copy.wait_recv()
             s["lx"][x] = functools.reduce(lambda a, b: a + b, [s["ly"][k] for k in range(ny)])
             lx_copies.extend(send(s["lx"].at[x], s["lx"].at[x], s["lx_sem"], e - 1, xpeer(e)) for e in range(1, nx))
 
-    hidden_grad = ring_reduce(s["hp"], s["h_rbox"], s["h_lbox"], (s["pr_sem"], s["pl_sem"]),
-                              min(2, grp), down_between)
-    s["gr"][z, 0] = (hidden_grad * s["slope"][...]).astype(BF16)
-    s["gr"][z, 1] = (hidden_grad * s["silu"][...]).astype(BF16)
+    hidden_grad = skip_reduce(s["hp"], s["h_stage"], (s["h_rbox"], s["h_lbox"]),
+                              (s["pr_sem"], s["pl_sem"]), down_between)[:, 0:ff]
+    s["gr"][z, :, 0:ff] = (hidden_grad * s["slope"][...]).astype(BF16)
+    s["gr"][z, :, ff:2 * ff] = (hidden_grad * s["silu"][...]).astype(BF16)
 
     def loss_finish(step):
         if step == 1:
             for copy in lx_copies:
                 copy.wait_recv()
-            loss_o[...] = functools.reduce(lambda a, b: a + b, [s["lx"][k] for k in range(nx)])
-
-    ring_gather(s["gr"], (s["wr_sem"], s["wl_sem"]), loss_finish)
+            loss = functools.reduce(lambda a, b: a + b, [s["lx"][k] for k in range(nx)])
+            loss_o[...] = loss[0:1, 0:1]
+
+    ring_gather(s["gr"], (s["wr_sem"], s["wl_sem"]), WSUB, loss_finish)
 
     outs = []
-    for k, (buf, dst) in enumerate(((s["gg"], gg_o), (s["gu"], gu_o))):
-        grads = flat(s["gr"][:, k])
-        for h in range(2):
-            buf[h * half:(h + 1) * half, :] = lax.dot_general(
-                flat(s["tok"][h]), grads, tn, preferred_element_type=F32).astype(BF16)
-            at = pl.ds(h * half, half)
-            out = pltpu.make_async_copy(buf.at[at], dst.at[at], s["out"].at[1 + 2 * k + h])
-            out.start()
-            outs.append(out)
+    grads = flat(s["gr"][...])
+    for h in range(2):
+        s["gw"][:, h * half:(h + 1) * half] = lax.dot_general(
+            grads, flat(s["tok"][h]), tn, preferred_element_type=F32).astype(BF16)
+    for k, dst in enumerate((gg_o, gu_o)):
+        out = pltpu.make_async_copy(s["gw"].at[k * ff:(k + 1) * ff], dst, s["out"].at[1 + k])
+        out.start()
+        outs.append(out)
     for copy in sent:
         copy.wait_send()
     loads[6].wait()
@@ -385,6 +461,8 @@
     half = d_in // 2
     tz = tokens // nz
     g = tz // 8
+    tg = tz // 16
+    ffp = -(-ff // 128) * 128
     V = pltpu.VMEM
 
     def sems(*n):
@@ -392,8 +470,7 @@
 
     vm = dict(
         si=V((8, d_in), BF16), th=V((tokens, k_in), BF16), proj=V((k_in, d_in), BF16),
-        wg=V((d_in, ff), BF16), wu=V((d_in, ff), BF16), wd=V((ff, d_in), BF16),
-        wcat=V((d_in, 2 * ff), BF16),
+        wcat=V((2 * ff, d_in), BF16), wd=V((ffp, d_in), BF16),
         pair_out=V((8, half), F32), pair=V((2, 8, half), F32),
         tok=V((2, ny, nx, 16, half), BF16), sg=V((2, ny, nx, 16, half), BF16),
         tp=V((2, ny, nx, 16, half), F32), sp=V((2, ny, nx, 16, half), F32),
@@ -403,32 +480,34 @@
         t_sum=V((ny, 16, half), F32), s_sum=V((ny, 16, half), F32),
         t_ybox=V((ny - 1, 16, half), F32), s_ybox=V((ny - 1, 16, half), F32),
         teach=V((16, half), F32),
-        gp=V((tokens // 8, 8, 2 * ff), F32), hp=V((tokens // 8, 8, ff), F32),
+        gp=V((tokens // 8, 8, 2 * ff), F32), hp=V((tokens // 16, 16, ffp), F32),
         g_rbox=V((zr, g, 8, 2 * ff), F32), g_lbox=V((zl, g, 8, 2 * ff), F32),
-        h_rbox=V((zr, g, 8, ff), F32), h_lbox=V((zl, g, 8, ff), F32),
-        hid=V((nz, tz, ff), BF16), gr=V((nz, 2, tz, ff), BF16),
+        h_rbox=V((zr, tg, 16, ffp), BF16), h_lbox=V((zl, tg, 16, ffp), BF16),
+        h_stage=V((2, zr, tg, 16, ffp), BF16),
+        hid=V((nz, tz, ffp), BF16), gr=V((nz, tz, 2 * ff), BF16),
         silu=V((tz, ff), F32), slope=V((tz, ff), F32),
-        st_pair=V((2, 16, 128), F32), st_z=V((nz, 16, 128), F32),
+        st_pair=V((2, 8, 128), F32), st_z=V((nz, 8, 128), F32),
         ly=V((ny, 8, 128), F32), lx=V((nx, 8, 128), F32),
-        gd=V((ff, d_in), BF16), gg=V((d_in, ff), BF16), gu=V((d_in, ff), BF16),
+        gd=V((ff, d_in), BF16), gw=V((2 * ff, d_in), BF16),
     )
-    gs, hs = NSUB, min(2, g)
+    gs = NSUB
     sm = dict(
         pair_sem=sems(1), tc_sem=sems(nx), sc_sem=sems(nx),
         txs_sem=sems(nx - 1), sxs_sem=sems(nx - 1), tys_sem=sems(ny - 1), sys_sem=sems(ny - 1),
         ty_sem=sems(ny - 1), tx_sem=sems(ny * (nx - 1)), tk_sem=sems(nx),
         gy_sem=sems(ny - 1), gx_sem=sems(ny * (nx - 1)), gk_sem=sems(nx),
         gr_sem=sems(zr * gs), gl_sem=sems(zl * gs), hr_sem=sems(zr), hl_sem=sems(zl),
-        pr_sem=sems(zr * hs), pl_sem=sems(zl * hs), wr_sem=sems(zr), wl_sem=sems(zl),
+        pr_sem=sems(zr), pl_sem=sems(zl), wr_sem=sems(zr * WSUB), wl_sem=sems(zl * WSUB),
         stc_sem=sems(1), stz_sem=sems(nz - 1), ly_sem=sems(ny - 1), lx_sem=sems(nx - 1),
-        load=DMA((6,)), out=DMA((5,)),
+        load=DMA((6,)), out=DMA((3,)),
     )
     return {**vm, **sm}
 
 
 def local(nz, ny, nx, student_in, teacher_hidden, proj, w_gate, w_up, w_down):
+    w_gate, w_up = w_gate.T, w_up.T
     d_in = student_in.shape[1]
-    ff = w_gate.shape[1]
+    ff = w_gate.shape[0]
     names = scratch(nz, ny, nx, d_in, proj.shape[0], ff)
     tree = jax.tree.structure(names)
     leaves = jax.tree.leaves(names)
@@ -441,8 +520,8 @@
     out = pl.pallas_call(
         kernel,
         out_shape=(
-            jax.ShapeDtypeStruct((d_in, ff), BF16), jax.ShapeDtypeStruct((d_in, ff), BF16),
-            jax.ShapeDtypeStruct((ff, d_in), BF16), jax.ShapeDtypeStruct((8, 128), F32)),
+            jax.ShapeDtypeStruct((ff, d_in), BF16), jax.ShapeDtypeStruct((ff, d_in), BF16),
+            jax.ShapeDtypeStruct((ff, d_in), BF16), jax.ShapeDtypeStruct((1, 1), F32)),
         in_specs=[any_spec] * 6,
         out_specs=(any_spec, any_spec, any_spec, pl.BlockSpec(memory_space=pltpu.VMEM)),
         scratch_shapes=leaves,
@@ -450,7 +529,7 @@
             collective_id=0, has_side_effects=True, vmem_limit_bytes=56 * 1024 * 1024),
         name="distill_step",
     )(student_in, teacher_hidden, proj, w_gate, w_up, w_down)
-    return out[0], out[1], out[2], out[3][0, 0]
+    return out[0].T, out[1].T, out[2], out[3].reshape(())
 
 
 def solution(mesh):

time: 197 us -> 170 us (0.86)
  the two profiles are of different devices: /device:TPU:8 before, /device:TPU:16 now
where the time goes in v2:
time: 170 us
  Pallas kernels  163 us (96%)
  local copies, waits for them, and re-layouts  3.82 us (2%)
  between operations  2.45 us (1%)
    pallas_call x1, Pallas kernels, local(): pl.pallas_call(kernel, out_shape=(jax.ShapeDtypeStruct((ff, d_in), BF16),...  163 us
    unnamed x7, local copies, waits for them, and re-layouts  3.82 us

profile of v2, /device:TPU:16, one launch (start us, length us, event | category | flops | bytes accessed | tf_op | source)
XLA Modules:
  0.0 169.6 jit_solution(2524806514504449294)
XLA Ops:
  0.6 163.4 %distill_step.1 = (bf16[448,512]{1,0:T(8,128)(2,1)}, bf16[448,512]{1,0:T(8,128)(2,1)}, bf16[448,512]{1,0:T(8,128)(2,1)}, f32[1,1]{1,0:T(1,128)}) custom-call(bf16[8,512]{1,0:T(8,128)(2,1)} %refs_0_.1, bf16[512,256]{1,0:T(8,128)(2,1)} %refs_1_.1, bf16[256,512]{1,0:T(8,128)(2,1)} %refs_2_.1, bf16[448,512]{1,0:T(8,128)(2,1)} %bitcast.7, ...), custom_call_target="tpu_custom_call" | custom-call | tf_op jit(solution)/shard_map/distill_step/pallas_call | solution.py:520
  164.0 0.0 copy-start.1
  164.0 1.9 %copy.14 = bf16[512,448]{0,1:T(8,128)(2,1)} copy(bf16[512,448]{0,1:T(8,128)(2,1)} %bitcast.6) | data formatting | bytes 917504
  165.9 0.0 copy-done.1
  165.9 0.0 copy-start
  165.9 0.8 copy.15
  166.7 0.4 copy-done
  167.1 0.8 copy.16
Async XLA Ops:
  164.0 1.9 %copy-start.1 = (bf16[448,512]{1,0:T(8,128)(2,1)S(1)}, bf16[448,512]{1,0:T(8,128)(2,1)}, u32[]{:S(2)}) copy-start(bf16[448,512]{1,0:T(8,128)(2,1)} %get-tuple-element.9) | copy-start | bytes 1376260
  165.9 1.2 copy-start

commit v3 on v2

--- a/solution.py
+++ b/solution.py
@@ -12,7 +12,6 @@
 MESH = pl.DeviceIdType.MESH
 DMA = pltpu.SemaphoreType.DMA
 NSUB = 4
-WSUB = 2
 
 
 def body(nz, ny, nx, si_h, th_h, proj_h, wg_h, wu_h, wd_h,
@@ -22,6 +21,7 @@
     tokens = ny * nx * 16
     grp = tokens // nz // 8
     tg = tokens // nz // 16
+    tz = tokens // nz
     ff = wg_h.shape[0]
     ffp = s["wd"].shape[0]
     half = si_h.shape[1] // 2
@@ -86,6 +86,7 @@
     if ffp > ff:
         s["wd"][ff:ffp, :] = jnp.zeros((ffp - ff, 2 * half), BF16)
         s["hid"][z, :, ff:ffp] = jnp.zeros((s["hid"].shape[1], ffp - ff), BF16)
+        s["ab"][z, :, ff:ffp] = jnp.zeros((s["ab"].shape[1], ffp - ff), BF16)
 
     loads[0].wait()
     own = s["si"][...].astype(F32)
@@ -175,8 +176,6 @@
     started = gather_start(s["tok"], tok_sems)
     gather_finish(s["tok"], tok_sems, started)
 
-    teach_x = x_stage(s["tp"], s["t_in"], s["t_out"], s["t_box"], s["txs_sem"], teach_pair)
-
     loads[3].wait()
     loads[4].wait()
     yrow = ny // nrow
@@ -196,58 +195,37 @@
         size = grp // nsub
 
         def chunk(j, q):
-            return pl.ds(wrap(j, nz) * grp + q * size, size)
-
-        def piece(q):
-            return pl.ds(q * size, size)
-
+            return (pl.ds(wrap(j, nz) * grp + q // 2 * size, size), slice(None), lanes[q % 2])
+
+        def piece(step, q):
+            return (step, pl.ds(q // 2 * size, size), slice(None), lanes[q % 2])
+
+        width = part.shape[2]
+        cut = -(-width // 256) * 128
+        lanes = (slice(0, cut), slice(cut, width))
         r_copies, l_copies = [], []
-        for q in range(nsub):
-            r_copies.append(send(part.at[chunk(z + zr, q)], rbox.at[0, piece(q)], r_sems, q, right))
-            l_copies.append(send(part.at[chunk(z - zl, q)], lbox.at[0, piece(q)], l_sems, q, left))
+        for q in range(2 * nsub):
+            r_copies.append(send(part.at[chunk(z + zr, q)], rbox.at[piece(0, q)], r_sems, q, right))
+            l_copies.append(send(part.at[chunk(z - zl, q)], lbox.at[piece(0, q)], l_sems, q, left))
         for step in range(1, zr):
             between(step)
-            for q in range(nsub):
+            for q in range(2 * nsub):
+                was, now = piece(step - 1, q), piece(step, q)
+                at = step * 2 * nsub + q
                 r_copies[q].wait_recv()
-                rbox[step - 1, piece(q)] = rbox[step - 1, piece(q)] + part[chunk(z + zr - step, q)]
-                r_copies[q] = send(rbox.at[step - 1, piece(q)], rbox.at[step, piece(q)],
-                                   r_sems, step * nsub + q, right)
+                rbox[was] = rbox[was] + part[chunk(z + zr - step, q)]
+                r_copies[q] = send(rbox.at[was], rbox.at[now], r_sems, at, right)
                 if step < zl:
                     l_copies[q].wait_recv()
-                    lbox[step - 1, piece(q)] = lbox[step - 1, piece(q)] + part[chunk(z - zl + step, q)]
-                    l_copies[q] = send(lbox.at[step - 1, piece(q)], lbox.at[step, piece(q)],
-                                       l_sems, step * nsub + q, left)
-        for q in range(nsub):
+                    lbox[was] = lbox[was] + part[chunk(z - zl + step, q)]
+                    l_copies[q] = send(lbox.at[was], lbox.at[now], l_sems, at, left)
+        for q in range(2 * nsub):
             l_copies[q].wait_recv()
             r_copies[q].wait_recv()
         total = part[pl.ds(z * grp, grp)] + rbox[zr - 1] + lbox[zl - 1]
         return flat(total)
 
-    def ring_gather(buf, sems, nsub, between):
-        r_sems, l_sems = sems
-        size = buf.shape[1] // nsub
-
-        def part(k, q):
-            return buf.at[k, pl.ds(q * size, size)]
-
-        r_copies, l_copies = [], []
-        for q in range(nsub):
-            r_copies.append(send(part(z, q), part(z, q), r_sems, q, right))
-            l_copies.append(send(part(z, q), part(z, q), l_sems, q, left))
-        for step in range(1, zr + 1):
-            for q in range(nsub):
-                r_copies[q].wait_recv()
-                if step < zr:
-                    block = part(wrap(z - step, nz), q)
-                    r_copies[q] = send(block, block, r_sems, step * nsub + q, right)
-                if step <= zl:
-                    l_copies[q].wait_recv()
-                    if step < zl:
-                        block = part(wrap(z + step, nz), q)
-                        l_copies[q] = send(block, block, l_sems, step * nsub + q, left)
-            between(step)
-
-    def skip_gather(buf, sems, between):
+    def skip_gather(buf, sems):
         copies = [{}, {}]
         sides = ((0, 1, zr), (1, -1, zl))
 
@@ -260,12 +238,13 @@
 
         for side in sides:
             spread(*side, 0)
+        yield
         for distance in range(2, zr + 1, 2):
             for side, sign, reach in sides:
                 if distance <= reach:
                     copies[side][distance].wait_recv()
                     spread(side, sign, reach, distance)
-            between(distance // 2)
+            yield
         for side, sign, reach in sides:
             for distance in range(1, reach + 1, 2):
                 copies[side][distance].wait_recv()
@@ -310,9 +289,11 @@
             total = total + arrived(side, reach, 0)
         return flat(total)
 
-    y_copies = []
+    teach_x, y_copies = [], []
 
     def teach_between(step):
+        if step == 1:
+            teach_x.extend(x_stage(s["tp"], s["t_in"], s["t_out"], s["t_box"], s["txs_sem"], teach_pair))
         if step == zr - 1:
             y_copies.extend(y_stage(s["t_out"], s["t_box"], s["t_sum"], s["t_ybox"], s["tys_sem"], teach_x))
 
@@ -322,15 +303,16 @@
     logistic = 1.0 / (1.0 + jnp.exp(-gate_val))
     silu_gate = gate_val * logistic
     s["hid"][z, :, 0:ff] = (silu_gate * up_val).astype(BF16)
-    s["silu"][...] = silu_gate
-    s["slope"][...] = up_val * (logistic * (1.0 + gate_val * (1.0 - logistic)))
-
-    def teach_finish(step):
-        if step == 1:
-            s["teach"][...] = y_total(s["t_sum"], s["t_ybox"], y_copies)
-
+    gather = skip_gather(s["hid"], (s["hr_sem"], s["hl_sem"]))
+    next(gather)
+    slope = up_val * (logistic * (1.0 + gate_val * (1.0 - logistic)))
+    s["ab"][z, 0:tz, 0:ff] = slope.astype(BF16)
+    s["ab"][z, tz:2 * tz, 0:ff] = silu_gate.astype(BF16)
     loads[5].wait()
-    skip_gather(s["hid"], (s["hr_sem"], s["hl_sem"]), teach_finish)
+    next(gather)
+    s["teach"][...] = y_total(s["t_sum"], s["t_ybox"], y_copies)
+    for _ in gather:
+        pass
 
     zrow = nz // nrow
 
@@ -344,11 +326,40 @@
 
         lax.fori_loop(0, nrow, tile, 0)
 
+    factors = skip_gather(s["ab"], (s["ar_sem"], s["al_sem"]))
+    order = sorted(range(ny), key=lambda d: -min(d, ny - d))
     stud_half(other)
-    stud_pair = pair_stage(s["sp"], s["s_in"], s["sc_sem"])
+    pair_copies = {}
+    for d in order:
+        yy = wrap(y + d, ny)
+        pair_copies[d] = send(s["sp"].at[other, yy], s["s_in"].at[yy], s["sc_sem"], d, partner)
+    next(factors)
     stud_half(core)
-    stud_x = x_stage(s["sp"], s["s_in"], s["s_out"], s["s_box"], s["sxs_sem"], stud_pair)
-    stud_y = y_stage(s["s_out"], s["s_box"], s["s_sum"], s["s_ybox"], s["sys_sem"], stud_x)
+    x_copies = {}
+    for d in order:
+        yy = wrap(y + d, ny)
+        pair_copies[d].wait_recv()
+        x_copies[d] = []
+        for e in range(1, nx):
+            xx = wrap(x + e, nx)
+            s["s_out"][e, yy] = s["sp"][core, yy, xx] + s["s_in"][yy, xx]
+            x_copies[d].append(send(s["s_out"].at[e, yy], s["s_box"].at[e - 1, yy], s["sxs_sem"],
+                                    d * (nx - 1) + e - 1, xpeer(e)))
+        s["s_out"][0, yy] = s["sp"][core, yy, x] + s["s_in"][yy, x]
+    next(factors)
+    stud_y = []
+    for d in order:
+        yy = wrap(y + d, ny)
+        total = s["s_out"][0, yy]
+        for e in range(1, nx):
+            x_copies[d][e - 1].wait_recv()
+            total = total + s["s_box"][e - 1, yy]
+        s["s_sum"][yy] = total
+        if d:
+            stud_y.append((d, send(s["s_sum"].at[yy], s["s_ybox"].at[d - 1], s["sys_sem"], d - 1, ypeer(d))))
+    stud_y = [copy for _, copy in sorted(stud_y, key=lambda pair: pair[0])]
+    if zr > 2:
+        next(factors)
 
     teacher = s["teach"][...]
     teach_max = jnp.max(teacher, axis=1, keepdims=True)
@@ -364,23 +375,32 @@
     stats = jnp.where(lane == 0, stud_max, jnp.where(lane == 1, teach_max, jnp.where(
         lane == 2, stud_norm, jnp.where(lane == 3, teach_norm, cross))))
     stats = jnp.concatenate([stats, jnp.zeros((112, 128), F32)], axis=0).T[0:8]
-    row = lax.broadcasted_iota(jnp.int32, (8, 128), 0)
-
-    def join(tiles):
-        top = functools.reduce(jnp.maximum, tiles)
-        total = jnp.zeros((8, 128), F32)
-        for tile in tiles:
-            scale = jnp.exp(tile - top)
-            total += tile * jnp.where(row == 2, scale[0:1], scale[1:2])
-        return jnp.where(row < 2, top, total)
-
-    s["st_pair"][core] = stats
-    send(s["st_pair"].at[core], s["st_pair"].at[core], s["stc_sem"], 0, partner).wait_recv()
-    s["st_z"][z] = join([s["st_pair"][0], s["st_pair"][1]])
-    st_copies = [send(s["st_z"].at[z], s["st_z"].at[z], s["stz_sem"], d - 1, zpeer(d)) for d in range(1, nz)]
+    line = stats[0:1]
+    for k in range(1, 5):
+        line = line + pltpu.roll(stats, 16 * k, 1)[k:k + 1]
+    mine = 2 * z + core
+    s["st"][mine] = line
+    st_copies = []
+    for d in range(nz):
+        for k, cc in enumerate((core, other)):
+            if d or k:
+                st_copies.append(send(s["st"].at[mine], s["st"].at[mine], s["st_sem"], 2 * d + k - 1,
+                                      (wrap(z + d, nz), col(y, x, cc))))
+    if zr > 3:
+        next(factors)
     for copy in st_copies:
         copy.wait_recv()
-    stats = join([s["st_z"][k] for k in range(nz)])
+    lines = s["st"][...].reshape((2 * nz, 128))
+    top = jnp.max(lines, axis=0, keepdims=True)
+    scale = jnp.exp(lines - top)
+    wide = lax.broadcasted_iota(jnp.int32, (2 * nz, 128), 1)
+    scale = jnp.where(wide < 64, pltpu.roll(scale, 32, 1), pltpu.roll(scale, 48, 1))
+    total = jnp.sum(lines * scale, axis=0, keepdims=True)
+    row = lax.broadcasted_iota(jnp.int32, (8, 128), 0)
+    line = jnp.broadcast_to(jnp.where(wide[0:1] < 32, top, total), (8, 128))
+    stats = line
+    for k in range(1, 5):
+        stats = jnp.where(row == k, pltpu.roll(line, 128 - 16 * k, 1), stats)
     stats = jnp.concatenate([stats, jnp.zeros((120, 128), F32)], axis=0).T[0:16]
     stud_max = stats[:, 0:1]
     teach_max = stats[:, 1:2]
@@ -411,40 +431,53 @@
     lx_copies = []
 
     def down_between(step):
-        if step == 1:
-            for h in range(2):
-                s["gd"][:, h * half:(h + 1) * half] = lax.dot_general(
-                    flat(s["hid"][...]), flat(s["sg"][h]), tn, preferred_element_type=F32).astype(BF16)[0:ff]
-            out = pltpu.make_async_copy(s["gd"], gd_o, s["out"].at[0])
-            out.start()
-            loads.append(out)
-        if step == max(1, zr // 2 - 1):
+        if step <= 2:
+            h = step - 1
+            s["gd"][:, h * half:(h + 1) * half] = lax.dot_general(
+                flat(s["hid"][...]), flat(s["sg"][h]), tn, preferred_element_type=F32).astype(BF16)[0:ff]
+        if step == zr // 2:
             for copy in ly_copies:
                 copy.wait_recv()
             s["lx"][x] = functools.reduce(lambda a, b: a + b, [s["ly"][k] for k in range(ny)])
             lx_copies.extend(send(s["lx"].at[x], s["lx"].at[x], s["lx_sem"], e - 1, xpeer(e)) for e in range(1, nx))
 
     hidden_grad = skip_reduce(s["hp"], s["h_stage"], (s["h_rbox"], s["h_lbox"]),
-                              (s["pr_sem"], s["pl_sem"]), down_between)[:, 0:ff]
-    s["gr"][z, :, 0:ff] = (hidden_grad * s["slope"][...]).astype(BF16)
-    s["gr"][z, :, ff:2 * ff] = (hidden_grad * s["silu"][...]).astype(BF16)
-
-    def loss_finish(step):
-        if step == 1:
-            for copy in lx_copies:
-                copy.wait_recv()
-            loss = functools.reduce(lambda a, b: a + b, [s["lx"][k] for k in range(nx)])
-            loss_o[...] = loss[0:1, 0:1]
-
-    ring_gather(s["gr"], (s["wr_sem"], s["wl_sem"]), WSUB, loss_finish)
+                              (s["pr_sem"], s["pl_sem"]), down_between)
+    s["hg"][z] = hidden_grad.astype(BF16)
+    gather = skip_gather(s["hg"], (s["wr_sem"], s["wl_sem"]))
+    next(gather)
+    for _ in factors:
+        pass
+    if zr < 4:
+        for h in range(zr // 2, 2):
+            down_between(h + 1)
+    out = pltpu.make_async_copy(s["gd"], gd_o, s["out"].at[0])
+    out.start()
+    loads.append(out)
+    next(gather)
+    for copy in lx_copies:
+        copy.wait_recv()
+    loss = functools.reduce(lambda a, b: a + b, [s["lx"][k] for k in range(nx)])
+    loss_o[...] = loss[0:1, 0:1]
+    for _ in gather:
+        pass
+
+    def factor_tile(m, carry):
+        at = pl.ds(m * zrow, zrow)
+        grad = s["hg"][at].astype(F32)
+        for k in range(2):
+            factor = s["ab"][at, k * tz:(k + 1) * tz].astype(F32)
+            s["gr"][k, at] = (grad * factor).astype(BF16)
+        return carry
+
+    lax.fori_loop(0, nrow, factor_tile, 0)
 
     outs = []
-    grads = flat(s["gr"][...])
-    for h in range(2):
-        s["gw"][:, h * half:(h + 1) * half] = lax.dot_general(
-            grads, flat(s["tok"][h]), tn, preferred_element_type=F32).astype(BF16)
     for k, dst in enumerate((gg_o, gu_o)):
-        out = pltpu.make_async_copy(s["gw"].at[k * ff:(k + 1) * ff], dst, s["out"].at[1 + k])
+        for h in range(2):
+            s["gw"][k, :, h * half:(h + 1) * half] = lax.dot_general(
+                flat(s["gr"][k]), flat(s["tok"][h]), tn, preferred_element_type=F32).astype(BF16)[0:ff]
+        out = pltpu.make_async_copy(s["gw"].at[k], dst, s["out"].at[1 + k])
         out.start()
         outs.append(out)
     for copy in sent:
@@ -484,21 +517,22 @@
         g_rbox=V((zr, g, 8, 2 * ff), F32), g_lbox=V((zl, g, 8, 2 * ff), F32),
         h_rbox=V((zr, tg, 16, ffp), BF16), h_lbox=V((zl, tg, 16, ffp), BF16),
         h_stage=V((2, zr, tg, 16, ffp), BF16),
-        hid=V((nz, tz, ffp), BF16), gr=V((nz, tz, 2 * ff), BF16),
-        silu=V((tz, ff), F32), slope=V((tz, ff), F32),
-        st_pair=V((2, 8, 128), F32), st_z=V((nz, 8, 128), F32),
+        hid=V((nz, tz, ffp), BF16), hg=V((nz, tz, ffp), BF16),
+        ab=V((nz, 2 * tz, ffp), BF16), gr=V((2, nz, tz, ffp), BF16),
+        st=V((2 * nz, 1, 128), F32),
         ly=V((ny, 8, 128), F32), lx=V((nx, 8, 128), F32),
-        gd=V((ff, d_in), BF16), gw=V((2 * ff, d_in), BF16),
+        gd=V((ff, d_in), BF16), gw=V((2, ff, d_in), BF16),
     )
     gs = NSUB
     sm = dict(
-        pair_sem=sems(1), tc_sem=sems(nx), sc_sem=sems(nx),
-        txs_sem=sems(nx - 1), sxs_sem=sems(nx - 1), tys_sem=sems(ny - 1), sys_sem=sems(ny - 1),
+        pair_sem=sems(1), tc_sem=sems(nx), sc_sem=sems(ny),
+        txs_sem=sems(nx - 1), sxs_sem=sems(ny * (nx - 1)), tys_sem=sems(ny - 1), sys_sem=sems(ny - 1),
         ty_sem=sems(ny - 1), tx_sem=sems(ny * (nx - 1)), tk_sem=sems(nx),
         gy_sem=sems(ny - 1), gx_sem=sems(ny * (nx - 1)), gk_sem=sems(nx),
-        gr_sem=sems(zr * gs), gl_sem=sems(zl * gs), hr_sem=sems(zr), hl_sem=sems(zl),
-        pr_sem=sems(zr), pl_sem=sems(zl), wr_sem=sems(zr * WSUB), wl_sem=sems(zl * WSUB),
-        stc_sem=sems(1), stz_sem=sems(nz - 1), ly_sem=sems(ny - 1), lx_sem=sems(nx - 1),
+        gr_sem=sems(2 * zr * gs), gl_sem=sems(2 * zl * gs), hr_sem=sems(zr), hl_sem=sems(zl),
+        pr_sem=sems(zr), pl_sem=sems(zl), wr_sem=sems(zr), wl_sem=sems(zl),
+        ar_sem=sems(zr), al_sem=sems(zl),
+        st_sem=sems(2 * nz - 1), ly_sem=sems(ny - 1), lx_sem=sems(nx - 1),
         load=DMA((6,)), out=DMA((3,)),
     )
     return {**vm, **sm}

time: 170 us -> 157 us (0.924)
  the two profiles are of different devices: /device:TPU:16 before, /device:TPU:64 now
where the time goes in v3:
time: 157 us
  Pallas kernels  150 us (96%)
  local copies, waits for them, and re-layouts  3.82 us (2%)
  between operations  2.45 us (2%)
    pallas_call x1, Pallas kernels, local(): pl.pallas_call(kernel, out_shape=(jax.ShapeDtypeStruct((ff, d_in), BF16),...  150 us
    unnamed x7, local copies, waits for them, and re-layouts  3.82 us

profile of v3, /device:TPU:64, one launch (start us, length us, event | category | flops | bytes accessed | tf_op | source)
XLA Modules:
  0.0 156.7 jit_solution(17555349254576133996)
XLA Ops:
  0.6 150.4 %distill_step.1 = (bf16[448,512]{1,0:T(8,128)(2,1)}, bf16[448,512]{1,0:T(8,128)(2,1)}, bf16[448,512]{1,0:T(8,128)(2,1)}, f32[1,1]{1,0:T(1,128)}) custom-call(bf16[8,512]{1,0:T(8,128)(2,1)} %refs_0_.1, bf16[512,256]{1,0:T(8,128)(2,1)} %refs_1_.1, bf16[256,512]{1,0:T(8,128)(2,1)} %refs_2_.1, bf16[448,512]{1,0:T(8,128)(2,1)} %bitcast.7, ...), custom_call_target="tpu_custom_call" | custom-call | tf_op jit(solution)/shard_map/distill_step/pallas_call | solution.py:554
  151.1 0.0 copy-start.1
  151.1 1.9 %copy.14 = bf16[512,448]{0,1:T(8,128)(2,1)} copy(bf16[512,448]{0,1:T(8,128)(2,1)} %bitcast.6) | data formatting | bytes 917504
  153.0 0.0 copy-done.1
  153.0 0.0 copy-start
  153.0 0.8 copy.15
  153.7 0.4 copy-done
  154.1 0.8 copy.16
Async XLA Ops:
  151.1 1.9 %copy-start.1 = (bf16[448,512]{1,0:T(8,128)(2,1)S(1)}, bf16[448,512]{1,0:T(8,128)(2,1)}, u32[]{:S(2)}) copy-start(bf16[448,512]{1,0:T(8,128)(2,1)} %get-tuple-element.9) | copy-start | bytes 1376260
  153.0 1.2 copy-start

commit v4 on v3

--- a/solution.py
+++ b/solution.py
@@ -195,23 +195,20 @@
         size = grp // nsub
 
         def chunk(j, q):
-            return (pl.ds(wrap(j, nz) * grp + q // 2 * size, size), slice(None), lanes[q % 2])
+            return pl.ds(wrap(j, nz) * grp + q * size, size)
 
         def piece(step, q):
-            return (step, pl.ds(q // 2 * size, size), slice(None), lanes[q % 2])
-
-        width = part.shape[2]
-        cut = -(-width // 256) * 128
-        lanes = (slice(0, cut), slice(cut, width))
+            return (step, pl.ds(q * size, size))
+
         r_copies, l_copies = [], []
-        for q in range(2 * nsub):
+        for q in range(nsub):
             r_copies.append(send(part.at[chunk(z + zr, q)], rbox.at[piece(0, q)], r_sems, q, right))
             l_copies.append(send(part.at[chunk(z - zl, q)], lbox.at[piece(0, q)], l_sems, q, left))
         for step in range(1, zr):
             between(step)
-            for q in range(2 * nsub):
+            for q in range(nsub):
                 was, now = piece(step - 1, q), piece(step, q)
-                at = step * 2 * nsub + q
+                at = step * nsub + q
                 r_copies[q].wait_recv()
                 rbox[was] = rbox[was] + part[chunk(z + zr - step, q)]
                 r_copies[q] = send(rbox.at[was], rbox.at[now], r_sems, at, right)
@@ -219,7 +216,7 @@
                     l_copies[q].wait_recv()
                     lbox[was] = lbox[was] + part[chunk(z - zl + step, q)]
                     l_copies[q] = send(lbox.at[was], lbox.at[now], l_sems, at, left)
-        for q in range(2 * nsub):
+        for q in range(nsub):
             l_copies[q].wait_recv()
             r_copies[q].wait_recv()
         total = part[pl.ds(z * grp, grp)] + rbox[zr - 1] + lbox[zl - 1]
@@ -336,24 +333,39 @@
     next(factors)
     stud_half(core)
     x_copies = {}
+
+    def x_send(d, e, value, slot, device):
+        yy = wrap(y + d, ny)
+        s["s_out"][e, yy] = value
+        x_copies[d, slot] = send(s["s_out"].at[e, yy], s["s_box"].at[slot, yy], s["sxs_sem"], d * 3 + slot, device)
+
+    def x_own(d, e):
+        yy = wrap(y + d, ny)
+        xx = wrap(x + e, nx)
+        return s["sp"][core, yy, xx] + s["s_in"][yy, xx]
+
     for d in order:
-        yy = wrap(y + d, ny)
         pair_copies[d].wait_recv()
-        x_copies[d] = []
-        for e in range(1, nx):
-            xx = wrap(x + e, nx)
-            s["s_out"][e, yy] = s["sp"][core, yy, xx] + s["s_in"][yy, xx]
-            x_copies[d].append(send(s["s_out"].at[e, yy], s["s_box"].at[e - 1, yy], s["sxs_sem"],
-                                    d * (nx - 1) + e - 1, xpeer(e)))
-        s["s_out"][0, yy] = s["sp"][core, yy, x] + s["s_in"][yy, x]
+        if nx == 4:
+            x_send(d, 2, x_own(d, 2), 2, xpeer(1 if d % 2 == 0 else 3))
+            slot, e = (1, 3) if d % 2 == 0 else (0, 1)
+            x_send(d, e, x_own(d, e), slot, xpeer(e))
+        else:
+            x_send(d, 1, x_own(d, 1), 0, xpeer(1))
+        s["s_out"][0, wrap(y + d, ny)] = x_own(d, 0)
+    if nx == 4:
+        for d in order:
+            slot, e = (0, 1) if d % 2 == 0 else (1, 3)
+            x_copies[d, 2].wait_recv()
+            x_send(d, e, x_own(d, e) + s["s_box"][2, wrap(y + d, ny)], slot, xpeer(e))
     next(factors)
     stud_y = []
     for d in order:
         yy = wrap(y + d, ny)
         total = s["s_out"][0, yy]
-        for e in range(1, nx):
-            x_copies[d][e - 1].wait_recv()
-            total = total + s["s_box"][e - 1, yy]
+        for slot in range(2 if nx == 4 else 1):
+            x_copies[d, slot].wait_recv()
+            total = total + s["s_box"][slot, yy]
         s["s_sum"][yy] = total
         if d:
             stud_y.append((d, send(s["s_sum"].at[yy], s["s_ybox"].at[d - 1], s["sys_sem"], d - 1, ypeer(d))))
@@ -526,10 +538,10 @@
     gs = NSUB
     sm = dict(
         pair_sem=sems(1), tc_sem=sems(nx), sc_sem=sems(ny),
-        txs_sem=sems(nx - 1), sxs_sem=sems(ny * (nx - 1)), tys_sem=sems(ny - 1), sys_sem=sems(ny - 1),
+        txs_sem=sems(nx - 1), sxs_sem=sems(ny * 3), tys_sem=sems(ny - 1), sys_sem=sems(ny - 1),
         ty_sem=sems(ny - 1), tx_sem=sems(ny * (nx - 1)), tk_sem=sems(nx),
         gy_sem=sems(ny - 1), gx_sem=sems(ny * (nx - 1)), gk_sem=sems(nx),
-        gr_sem=sems(2 * zr * gs), gl_sem=sems(2 * zl * gs), hr_sem=sems(zr), hl_sem=sems(zl),
+        gr_sem=sems(zr * gs), gl_sem=sems(zl * gs), hr_sem=sems(zr), hl_sem=sems(zl),
         pr_sem=sems(zr), pl_sem=sems(zl), wr_sem=sems(zr), wl_sem=sems(zl),
         ar_sem=sems(zr), al_sem=sems(zl),
         st_sem=sems(2 * nz - 1), ly_sem=sems(ny - 1), lx_sem=sems(nx - 1),
@@ -569,7 +581,7 @@
 def solution(mesh):
     nz = mesh.shape["row"]
     chips = mesh.shape["col"] // 2
-    nx = 4 if chips == 32 else 2
+    nx = 4 if chips % 8 == 0 else 2
     ny = chips // nx
     return jax.shard_map(
         functools.partial(local, nz, ny, nx),

time: 157 us -> 159 us (1.013)
  the two profiles are of different devices: /device:TPU:64 before, /device:TPU:8 now
where the time goes in v4:
time: 159 us; the launch traced here: 158 us
  Pallas kernels  152 us (96%)
  local copies, waits for them, and re-layouts  3.82 us (2%)
  between operations  2.45 us (2%)
    pallas_call x1, Pallas kernels, local(): pl.pallas_call(kernel, out_shape=(jax.ShapeDtypeStruct((ff, d_in), BF16),...  152 us
    unnamed x7, local copies, waits for them, and re-layouts  3.82 us

profile of v4, /device:TPU:8, one launch (start us, length us, event | category | flops | bytes accessed | tf_op | source)
XLA Modules:
  0.0 158.4 jit_solution(911738932209123958)
XLA Ops:
  0.6 152.2 %distill_step.1 = (bf16[448,512]{1,0:T(8,128)(2,1)}, bf16[448,512]{1,0:T(8,128)(2,1)}, bf16[448,512]{1,0:T(8,128)(2,1)}, f32[1,1]{1,0:T(1,128)}) custom-call(bf16[8,512]{1,0:T(8,128)(2,1)} %refs_0_.1, bf16[512,256]{1,0:T(8,128)(2,1)} %refs_1_.1, bf16[256,512]{1,0:T(8,128)(2,1)} %refs_2_.1, bf16[448,512]{1,0:T(8,128)(2,1)} %bitcast.7, ...), custom_call_target="tpu_custom_call" | custom-call | tf_op jit(solution)/shard_map/distill_step/pallas_call | solution.py:566
  152.8 0.0 copy-start.1
  152.8 1.9 %copy.14 = bf16[512,448]{0,1:T(8,128)(2,1)} copy(bf16[512,448]{0,1:T(8,128)(2,1)} %bitcast.6) | data formatting | bytes 917504
  154.7 0.0 copy-done.1
  154.7 0.0 copy-start
  154.7 0.8 copy.15
  155.5 0.4 copy-done
  155.9 0.8 copy.16
Async XLA Ops:
  152.8 1.9 %copy-start.1 = (bf16[448,512]{1,0:T(8,128)(2,1)S(1)}, bf16[448,512]{1,0:T(8,128)(2,1)}, u32[]{:S(2)}) copy-start(bf16[448,512]{1,0:T(8,128)(2,1)} %get-tuple-element.9) | copy-start | bytes 1376260
  154.7 1.2 copy-start
